TPU v7x, 32 devices: a whole 2x2x4 slice. The times are simulated.
32 devices in a mesh: src: 8 (over y, x, core), dst: 4 (over z).
Axes of the slice: x: 2, y: 2, z: 4, core: 2. Of those that a mesh axis runs over, the one named last changes fastest.
Arguments:
- raw: bfloat16 [4096, 256], P(('src', 'dst')), may hold values from -6 to 6
- enc_w1: bfloat16 [256, 512], replicated, may hold values from -0.375 to 0.375
- enc_w2: bfloat16 [512, 256], replicated, may hold values from -0.25 to 0.25
- block_weights: float32 [512, 128, 128], P(('src', 'dst')), may hold values from -0.125 to 0.125
- block_cols: int32 [512], P(('src', 'dst')), may hold values from 0 to 3, as said below
- noise: bfloat16 [3, 4096, 256], P(None, ('src', 'dst')), may hold values from -3 to 3
Outputs:
- encoded: bfloat16 [4096, 256], P(('src', 'dst'))
- hops: bfloat16 [3, 4096, 256], P(None, ('src', 'dst'))
Inputs may be any that keep to these rules, and one draw needn't show every extreme that they name: `block_cols`: entry b of each device's 16 entries belongs to row block b // 2; row blocks 2j and 2j+1 of a device together name every column block exactly once, each naming 4 // 2 distinct ones.
All inputs are finite; a program needn't handle non-finite values.
Results may differ from a plain program's by a relative error of at most 0.0058.
Values may be sent and summed in bfloat16 or wider, within the bound.
A program may use at most 128 MiB of HBM per device.

v0:
```python
import jax
import jax.numpy as jnp
from jax import lax
from jax.sharding import PartitionSpec as P

HOPS = 3


def normalize_rows(z):
    return (z * lax.rsqrt(jnp.mean(z * z, axis=-1, keepdims=True) + 1e-06)).astype(jnp.bfloat16)


def shards(raw, enc_w1, enc_w2, block_weights, block_cols, noise):
    hidden = jax.nn.silu(jnp.dot(raw, enc_w1, preferred_element_type=jnp.float32)).astype(
        jnp.bfloat16
    )
    encoded = normalize_rows(jnp.dot(hidden, enc_w2, preferred_element_type=jnp.float32))
    own_rows = raw.shape[0]
    block_side = block_weights.shape[1]
    width = encoded.shape[1]
    feats = encoded
    kept = []
    for step in range(HOPS):
        group = lax.all_gather(feats, "dst", axis=0, tiled=True)
        col_count = group.shape[0] // block_side
        half = col_count // 2
        col_blocks = group.astype(jnp.float32).reshape(col_count, block_side, width)
        fetched = jnp.take(col_blocks, block_cols, axis=0)
        prods = jnp.einsum("bij,bjw->biw", block_weights, fetched, precision=lax.Precision.HIGHEST)
        mine = lax.psum_scatter(
            prods.reshape(own_rows * lax.axis_size("src") // block_side, half, block_side, width)
            .sum(axis=1)
            .reshape(own_rows * lax.axis_size("src"), width),
            "src",
            scatter_dimension=0,
            tiled=True,
        )
        feats = normalize_rows(mine + noise[step].astype(jnp.float32))
        kept.append(feats)
    return (encoded, jnp.stack(kept))


def solution(mesh):
    placed = (
        P(("src", "dst"), None),
        P(),
        P(),
        P(("src", "dst"), None, None),
        P(("src", "dst")),
        P(None, ("src", "dst"), None),
    )
    return jax.shard_map(
        shards,
        mesh=mesh,
        in_specs=placed,
        out_specs=(P(("src", "dst"), None), P(None, ("src", "dst"), None)),
        check_vma=False,
    )
```

profile of v0, /device:TPU:0, one launch (start us, length us, event | category | flops | bytes accessed | tf_op | source)
XLA Modules:
  0.0 204.7 jit_solution(9608763618662152512)
XLA Ops:
  7.2 0.0 copy-start
  7.2 0.0 reduce-scatter.4.cloned.1.call-start
  7.2 0.7 compare_and_fusion
  8.0 0.7 compare_select_fusion
  8.6 1.5 multiply_reduce_fusion.3
  10.1 0.1 multiply_convert_fusion.4
  10.2 0.0 copy-start.2
  10.2 15.7 %all_gather.9 = bf16[512,256]{1,0:T(8,128)(2,1)S(1)} all-gather(bf16[128,256]{1,0:T(8,128)(2,1)S(1)} %multiply_convert_fusion.4), channel_id=1, replica_groups=mesh['src'=8,'dst'=4] {'dst'}, dimensions={0}, use_global_device_ids=true | all-gather | bytes 327680 | tf_op jit(solution)/shard_map/all_gather | solution.py:24
  25.9 2.0 gather_fusion
  28.0 0.0 copy-done.2
  28.0 0.0 copy-done
  28.0 5.4 %bitcast_reduce_fusion.2 = f32[8,128,256]{1,2,0:T(8,128)S(1)} fusion(f32[16,128,128]{2,1,0:T(8,128)S(1)} %copy-done, f32[16,128,256]{2,1,0:T(8,128)} %gather_fusion, pred[16]{0:T(512)(128)(4,1)S(1)} %compare_and_fusion), kind=kOutput, calls=%fused_computation.5 | convolution fusion | flops 806092800 | bytes 4194320 | tf_op jit(solution)/shard_map/bij,bjw->biw/dot_general | solution.py:29
  33.4 0.0 copy-start.1
  33.4 1.3 copy.15
  34.8 0.0 reduce-scatter.4.cloned.1.call-update
  34.8 0.0 reduce-scatter.6.cloned.1.call-start
  34.9 37.6 %reduce-scatter.4.cloned.1.call-done = f32[128,256]{1,0:T(8,128)} async-done(((f32[1024,256]{1,0:T(8,128)}), f32[128,256]{1,0:T(8,128)}) %reduce-scatter.4.cloned.1.call-update) | async-done | bytes 131088 | tf_op jit(solution)/shard_map/reduce_scatter | solution.py:30
  72.4 0.0 copy-done.1
  72.4 1.0 multiply_reduce_fusion.2
  73.5 1.0 multiply_convert_fusion.3
  74.5 13.8 %all_gather.10 = bf16[512,256]{1,0:T(8,128)(2,1)S(1)} all-gather(bf16[128,256]{1,0:T(8,128)(2,1)S(1)} %multiply_convert_fusion.3), channel_id=1, replica_groups=mesh['src'=8,'dst'=4] {'dst'}, dimensions={0}, use_global_device_ids=true | all-gather | bytes 327680 | tf_op jit(solution)/shard_map/all_gather | solution.py:24
  88.3 2.0 gather_fusion.1
  90.4 5.4 %bitcast_reduce_fusion.1 = f32[8,128,256]{1,2,0:T(8,128)S(1)} fusion(f32[16,128,128]{2,1,0:T(8,128)S(1)} %copy-done, f32[16,128,256]{2,1,0:T(8,128)} %gather_fusion.1, pred[16]{0:T(512)(128)(4,1)S(1)} %compare_and_fusion), kind=kOutput, calls=%fused_computation.4 | convolution fusion | flops 806092800 | bytes 4194320 | tf_op jit(solution)/shard_map/bij,bjw->biw/dot_general | solution.py:29
  95.8 1.3 copy.17
  97.2 0.0 reduce-scatter.6.cloned.1.call-update
  97.2 0.0 reduce-scatter.8.cloned.1.call-start
  97.2 36.7 %reduce-scatter.6.cloned.1.call-done = f32[128,256]{1,0:T(8,128)} async-done(((f32[1024,256]{1,0:T(8,128)}), f32[128,256]{1,0:T(8,128)}) %reduce-scatter.6.cloned.1.call-update) | async-done | bytes 131088 | tf_op jit(solution)/shard_map/reduce_scatter | solution.py:30
  133.9 1.0 multiply_reduce_fusion.1
  134.9 1.0 multiply_convert_fusion.2
  135.9 14.1 %all_gather.11 = bf16[512,256]{1,0:T(8,128)(2,1)S(1)} all-gather(bf16[128,256]{1,0:T(8,128)(2,1)S(1)} %multiply_convert_fusion.2), channel_id=1, replica_groups=mesh['src'=8,'dst'=4] {'dst'}, dimensions={0}, use_global_device_ids=true | all-gather | bytes 327680 | tf_op jit(solution)/shard_map/all_gather | solution.py:24
  150.0 2.0 gather_fusion.2
  152.1 5.4 %bitcast_reduce_fusion = f32[8,128,256]{1,2,0:T(8,128)S(1)} fusion(f32[16,128,128]{2,1,0:T(8,128)S(1)} %copy-done, f32[16,128,256]{2,1,0:T(8,128)} %gather_fusion.2, pred[16]{0:T(512)(128)(4,1)S(1)} %compare_and_fusion), kind=kOutput, calls=%fused_computation.3 | convolution fusion | flops 806092800 | bytes 4194320 | tf_op jit(solution)/shard_map/bij,bjw->biw/dot_general | solution.py:29
  157.5 1.3 copy.19
  158.8 0.0 reduce-scatter.8.cloned.1.call-update
  158.9 36.6 %reduce-scatter.8.cloned.1.call-done = f32[128,256]{1,0:T(8,128)} async-done(((f32[1024,256]{1,0:T(8,128)}), f32[128,256]{1,0:T(8,128)}) %reduce-scatter.8.cloned.1.call-update) | async-done | bytes 131088 | tf_op jit(solution)/shard_map/reduce_scatter | solution.py:30
  195.5 1.0 multiply_reduce_fusion
  196.5 1.0 fusion.19
  197.5 0.7 pad_maximum_fusion
  (8 shorter events, 0.1 us)
Async XLA Ops:
  7.2 20.8 %copy-start = (f32[16,128,128]{2,1,0:T(8,128)S(1)}, f32[16,128,128]{2,1,0:T(8,128)}, u32[]{:S(2)}) copy-start(f32[16,128,128]{2,1,0:T(8,128)} %param.11) | copy-start | bytes 3145732
  7.2 65.3 %reduce-scatter.4.cloned.1.call-start = ((), (), s32[]{:S(2)}) async-start(), calls=%async_computation.3 | async-start | bytes 1179648 | tf_op jit(solution)/shard_map/reduce_scatter | solution.py:30
  10.2 17.7 %copy-start.2 = (bf16[128,256]{1,0:T(8,128)(2,1)}, bf16[128,256]{1,0:T(8,128)(2,1)S(1)}, u32[]{:S(2)}) copy-start(bf16[128,256]{1,0:T(8,128)(2,1)S(1)} %multiply_convert_fusion.4) | copy-start | bytes 196612
  33.4 39.0 %copy-start.1 = (bf16[3,128,256]{2,1,0:T(8,128)(2,1)S(1)}, bf16[3,128,256]{2,1,0:T(8,128)(2,1)}, u32[]{:S(2)}) copy-start(bf16[3,128,256]{2,1,0:T(8,128)(2,1)} %param.13) | copy-start | bytes 589828
  34.8 99.1 %reduce-scatter.6.cloned.1.call-start = ((), (), s32[]{:S(2)}) async-start(), calls=%async_computation.4 | async-start | bytes 1179648 | tf_op jit(solution)/shard_map/reduce_scatter | solution.py:30
  97.2 98.3 %reduce-scatter.8.cloned.1.call-start = ((), (), s32[]{:S(2)}) async-start(), calls=%async_computation.5 | async-start | bytes 1179648 | tf_op jit(solution)/shard_map/reduce_scatter | solution.py:30
Sparse Core Ops, SparseCore 0:
  34.9 37.4 reduce-scatter.3
  97.3 36.5 reduce-scatter.5
  159.0 36.4 reduce-scatter.7
where the time goes:
time: 205 us
  waiting for transfers between devices  111 us (54%)
  blocking collectives  43.6 us (21%)
  matrix products  17.8 us (9%)
  between operations  13.9 us (7%)
  local copies, waits for them, and re-layouts  10.1 us (5%)
  other arithmetic  8.34 us (4%)
    reduce_scatter x3, waiting for transfers between devices, shards(): lax.psum_scatter(prods.reshape(own_rows * lax.axis_size('src') // block_s...  111 us
    all_gather x3, blocking collectives, shards(): group = lax.all_gather(feats, 'dst', axis=0, tiled=True)  43.6 us
    dot_general x3, matrix products, shards(): jnp.einsum('bij,bjw->biw', block_weights, fetched, precision=lax.Precisio...  16.3 us
    gather x3, local copies, waits for them, and re-layouts, shards(): fetched = jnp.take(col_blocks, block_cols, axis=0)  6.1 us
  transfers between devices with their start and end apart: 3, of which 3 were waited for; matrix products, arithmetic and copies ran while one was open for 0% of the time, Pallas kernels for 0%

commit v1 on v0

--- a/solution.py
+++ b/solution.py
@@ -4,6 +4,18 @@
 from jax.sharding import PartitionSpec as P
 
 HOPS = 3
+
+
+def doubled_up(x, axis, dim):
+    ways, here = (lax.axis_size(axis), lax.axis_index(axis))
+    grown, reach = (x, 1)
+    while reach < ways:
+        theirs = lax.ppermute(grown, axis, [(d, d ^ reach) for d in range(ways)])
+        mine_first = jnp.concatenate([grown, theirs], axis=dim)
+        theirs_first = jnp.concatenate([theirs, grown], axis=dim)
+        grown = jnp.where(here & reach == 0, mine_first, theirs_first)
+        reach = 2 * reach
+    return grown
 
 
 def normalize_rows(z):
@@ -21,7 +33,7 @@
     feats = encoded
     kept = []
     for step in range(HOPS):
-        group = lax.all_gather(feats, "dst", axis=0, tiled=True)
+        group = doubled_up(feats, "dst", 0)
         col_count = group.shape[0] // block_side
         half = col_count // 2
         col_blocks = group.astype(jnp.float32).reshape(col_count, block_side, width)

time: 205 us -> 196 us (0.956)
  blocking collectives: 43.6 us -> 0 us
  waiting for transfers between devices: 111 us -> 132 us
  starting transfers between devices: 0.12 us -> 14.5 us
    all_gather x3 -> x0, blocking collectives: 43.6 us -> none  [shards(): group = lax.all_gather(feats, 'dst', axis=0, tiled=True)]
    ppermute x0 -> x6, waiting for transfers between devices: none -> 22.3 us  [doubled_up(): theirs = lax.ppermute(grown, axis, [(d, d ^ reach) for d in range(ways)])]
    ppermute x0 -> x6, starting transfers between devices: none -> 14.2 us  [doubled_up(): theirs = lax.ppermute(grown, axis, [(d, d ^ reach) for d in range(ways)])]
  transfers between devices with their start and end apart: 3 -> 9, of which waited for: 3 -> 9; matrix products, arithmetic and copies ran while one was open for 0% -> 0% of each run, Pallas kernels for 0% -> 0%
where the time goes in v1:
time: 196 us
  waiting for transfers between devices  132 us (67%)
  matrix products  17.9 us (9%)
  starting transfers between devices  14.5 us (7%)
  between operations  13.9 us (7%)
  local copies, waits for them, and re-layouts  10.1 us (5%)
  other arithmetic  8.01 us (4%)
    reduce_scatter x3, waiting for transfers between devices, shards(): lax.psum_scatter(prods.reshape(own_rows * lax.axis_size('src') // block_s...  109 us
    ppermute x6, waiting for transfers between devices, doubled_up(): theirs = lax.ppermute(grown, axis, [(d, d ^ reach) for d in range(ways)])  22.3 us
    dot_general x3, matrix products, shards(): jnp.einsum('bij,bjw->biw', block_weights, fetched, precision=lax.Precisio...  16.3 us
    ppermute x6, starting transfers between devices, doubled_up(): theirs = lax.ppermute(grown, axis, [(d, d ^ reach) for d in range(ways)])  14.2 us
    gather x3, local copies, waits for them, and re-layouts, shards(): fetched = jnp.take(col_blocks, block_cols, axis=0)  6.1 us
    reduce_sum x3, local copies, waits for them, and re-layouts, shards(): mine = lax.psum_scatter(prods.reshape(own_rows * lax.axis_size('src') //...  3.98 us
  transfers between devices with their start and end apart: 9, of which 9 were waited for; matrix products, arithmetic and copies ran while one was open for 0% of the time, Pallas kernels for 0%

profile of v1, /device:TPU:0, one launch (start us, length us, event | category | flops | bytes accessed | tf_op | source)
XLA Modules:
  0.0 196.0 jit_solution(16013972075701003553)
XLA Ops:
  7.2 0.0 copy-start
  7.2 0.0 copy-start.3
  7.2 0.0 reduce-scatter.4.cloned.1.call-start
  7.2 1.6 multiply_reduce_fusion.3
  8.8 0.1 multiply_convert_fusion.4
  8.9 0.0 copy-start.2
  8.9 3.1 %collective-permute-start = (bf16[128,256]{1,0:T(8,128)(2,1)S(1)}, bf16[128,256]{1,0:T(8,128)(2,1)S(1)}, u32[]{:S(2)}, u32[]{:S(2)}) collective-permute-start(bf16[128,256]{1,0:T(8,128)(2,1)S(1)} %multiply_convert_fusion.4), channel_id=1, source_target_pairs={{0,1},{1,0},{2,3},{3,2},{4,5},{5,4},{6,7},{7,6},{8,9},{9,8},{10,11... | collective-permute-start | bytes 196616 | tf_op jit(solution)/shard_map/ppermute | solution.py:13
  12.0 0.7 compare_and_fusion
  12.7 1.6 collective-permute-done
  14.3 3.1 %collective-permute-start.1 = (bf16[256,256]{1,0:T(8,128)(2,1)S(1)}, bf16[256,256]{1,0:T(8,128)(2,1)S(1)}, u32[]{:S(2)}, u32[]{:S(2)}) collective-permute-start(bf16[256,256]{1,0:T(8,128)(2,1)S(1)} %maximum_select_fusion.3), channel_id=1, source_target_pairs={{0,2},{1,3},{2,0},{3,1},{4,6},{5,7},{6,4},{7,5},{8,10},{9,11},{10,... | collective-permute-start | bytes 393224 | tf_op jit(solution)/shard_map/ppermute | solution.py:13
  17.4 0.0 copy-done.3
  17.4 5.1 %collective-permute-done.1 = bf16[256,256]{1,0:T(8,128)(2,1)S(1)} collective-permute-done((bf16[256,256]{1,0:T(8,128)(2,1)S(1)}, bf16[256,256]{1,0:T(8,128)(2,1)S(1)}, u32[]{:S(2)}, u32[]{:S(2)}) %collective-permute-start.1) | collective-permute-done | bytes 131104 | tf_op jit(solution)/shard_map/ppermute | solution.py:13
  22.6 0.1 maximum_select_fusion
  22.7 2.0 %gather_fusion = f32[16,128,256]{2,1,0:T(8,128)} fusion(f32[4,128,256]{2,1,0:T(8,128)S(1)} %convert.6, s32[1024]{0:T(1024)S(1)} %pad_clamp_fusion), kind=kCustom, calls=%fused_computation.clone | custom fusion | bytes 4194368 | tf_op jit(solution)/shard_map/jit(_take)/gather | solution.py:40
  24.8 0.0 copy-done.2
  24.8 0.0 copy-done
  24.8 5.4 %bitcast_reduce_fusion.2 = f32[8,128,256]{1,2,0:T(8,128)S(1)} fusion(f32[16,128,128]{2,1,0:T(8,128)S(1)} %copy-done, f32[16,128,256]{2,1,0:T(8,128)} %gather_fusion, pred[16]{0:T(512)(128)(4,1)S(1)} %compare_and_fusion), kind=kOutput, calls=%fused_computation.5 | convolution fusion | flops 806092800 | bytes 4194320 | tf_op jit(solution)/shard_map/bij,bjw->biw/dot_general | solution.py:41
  30.2 0.0 copy-start.1
  30.2 1.3 copy.12
  31.6 0.0 reduce-scatter.4.cloned.1.call-update
  31.6 0.0 reduce-scatter.6.cloned.1.call-start
  31.6 37.2 %reduce-scatter.4.cloned.1.call-done = f32[128,256]{1,0:T(8,128)} async-done(((f32[1024,256]{1,0:T(8,128)}), f32[128,256]{1,0:T(8,128)}) %reduce-scatter.4.cloned.1.call-update) | async-done | bytes 131088 | tf_op jit(solution)/shard_map/reduce_scatter | solution.py:42
  68.9 0.0 copy-done.1
  68.9 1.0 multiply_reduce_fusion.2
  69.9 1.0 multiply_convert_fusion.3
  70.9 1.6 collective-permute-start.2
  72.5 2.8 %collective-permute-done.2 = bf16[128,256]{1,0:T(8,128)(2,1)S(1)} collective-permute-done((bf16[128,256]{1,0:T(8,128)(2,1)S(1)}, bf16[128,256]{1,0:T(8,128)(2,1)S(1)}, u32[]{:S(2)}, u32[]{:S(2)}) %collective-permute-start.2) | collective-permute-done | bytes 65568 | tf_op jit(solution)/shard_map/ppermute | solution.py:13
  75.2 2.5 %collective-permute-start.3 = (bf16[256,256]{1,0:T(8,128)(2,1)S(1)}, bf16[256,256]{1,0:T(8,128)(2,1)S(1)}, u32[]{:S(2)}, u32[]{:S(2)}) collective-permute-start(bf16[256,256]{1,0:T(8,128)(2,1)S(1)} %maximum_select_fusion.4), channel_id=1, source_target_pairs={{0,2},{1,3},{2,0},{3,1},{4,6},{5,7},{6,4},{7,5},{8,10},{9,11},{10,... | collective-permute-start | bytes 393224 | tf_op jit(solution)/shard_map/ppermute | solution.py:13
  77.7 5.0 %collective-permute-done.3 = bf16[256,256]{1,0:T(8,128)(2,1)S(1)} collective-permute-done((bf16[256,256]{1,0:T(8,128)(2,1)S(1)}, bf16[256,256]{1,0:T(8,128)(2,1)S(1)}, u32[]{:S(2)}, u32[]{:S(2)}) %collective-permute-start.3) | collective-permute-done | bytes 131104 | tf_op jit(solution)/shard_map/ppermute | solution.py:13
  82.7 0.1 maximum_select_fusion.1
  82.9 2.0 %gather_fusion.1 = f32[16,128,256]{2,1,0:T(8,128)} fusion(f32[4,128,256]{2,1,0:T(8,128)S(1)} %convert.8, s32[1024]{0:T(1024)S(1)} %pad_clamp_fusion), kind=kCustom, calls=%fused_computation.1.clone | custom fusion | bytes 4194368 | tf_op jit(solution)/shard_map/jit(_take)/gather | solution.py:40
  84.9 5.4 %bitcast_reduce_fusion.1 = f32[8,128,256]{1,2,0:T(8,128)S(1)} fusion(f32[16,128,128]{2,1,0:T(8,128)S(1)} %copy-done, f32[16,128,256]{2,1,0:T(8,128)} %gather_fusion.1, pred[16]{0:T(512)(128)(4,1)S(1)} %compare_and_fusion), kind=kOutput, calls=%fused_computation.4 | convolution fusion | flops 806092800 | bytes 4194320 | tf_op jit(solution)/shard_map/bij,bjw->biw/dot_general | solution.py:41
  90.4 1.3 copy.14
  91.7 0.0 reduce-scatter.6.cloned.1.call-update
  91.7 0.2 reduce-scatter.8.cloned.1.call-start
  92.0 35.9 %reduce-scatter.6.cloned.1.call-done = f32[128,256]{1,0:T(8,128)} async-done(((f32[1024,256]{1,0:T(8,128)}), f32[128,256]{1,0:T(8,128)}) %reduce-scatter.6.cloned.1.call-update) | async-done | bytes 131088 | tf_op jit(solution)/shard_map/reduce_scatter | solution.py:42
  127.8 1.0 multiply_reduce_fusion.1
  128.8 1.0 multiply_convert_fusion.2
  129.9 1.5 collective-permute-start.4
  131.4 2.8 %collective-permute-done.4 = bf16[128,256]{1,0:T(8,128)(2,1)S(1)} collective-permute-done((bf16[128,256]{1,0:T(8,128)(2,1)S(1)}, bf16[128,256]{1,0:T(8,128)(2,1)S(1)}, u32[]{:S(2)}, u32[]{:S(2)}) %collective-permute-start.4) | collective-permute-done | bytes 65568 | tf_op jit(solution)/shard_map/ppermute | solution.py:13
  134.2 2.5 %collective-permute-start.5 = (bf16[256,256]{1,0:T(8,128)(2,1)S(1)}, bf16[256,256]{1,0:T(8,128)(2,1)S(1)}, u32[]{:S(2)}, u32[]{:S(2)}) collective-permute-start(bf16[256,256]{1,0:T(8,128)(2,1)S(1)} %maximum_select_fusion.5), channel_id=1, source_target_pairs={{0,2},{1,3},{2,0},{3,1},{4,6},{5,7},{6,4},{7,5},{8,10},{9,11},{10,... | collective-permute-start | bytes 393224 | tf_op jit(solution)/shard_map/ppermute | solution.py:13
  136.7 5.0 %collective-permute-done.5 = bf16[256,256]{1,0:T(8,128)(2,1)S(1)} collective-permute-done((bf16[256,256]{1,0:T(8,128)(2,1)S(1)}, bf16[256,256]{1,0:T(8,128)(2,1)S(1)}, u32[]{:S(2)}, u32[]{:S(2)}) %collective-permute-start.5) | collective-permute-done | bytes 131104 | tf_op jit(solution)/shard_map/ppermute | solution.py:13
  141.7 0.1 maximum_select_fusion.2
  141.9 2.0 %gather_fusion.2 = f32[16,128,256]{2,1,0:T(8,128)} fusion(f32[4,128,256]{2,1,0:T(8,128)S(1)} %convert.10, s32[1024]{0:T(1024)S(1)} %pad_clamp_fusion), kind=kCustom, calls=%fused_computation.2.clone | custom fusion | bytes 4194368 | tf_op jit(solution)/shard_map/jit(_take)/gather | solution.py:40
  143.9 5.4 %bitcast_reduce_fusion = f32[8,128,256]{1,2,0:T(8,128)S(1)} fusion(f32[16,128,128]{2,1,0:T(8,128)S(1)} %copy-done, f32[16,128,256]{2,1,0:T(8,128)} %gather_fusion.2, pred[16]{0:T(512)(128)(4,1)S(1)} %compare_and_fusion), kind=kOutput, calls=%fused_computation.3 | convolution fusion | flops 806092800 | bytes 4194320 | tf_op jit(solution)/shard_map/bij,bjw->biw/dot_general | solution.py:41
  149.3 1.3 copy.16
  150.7 0.0 reduce-scatter.8.cloned.1.call-update
  150.7 36.1 %reduce-scatter.8.cloned.1.call-done = f32[128,256]{1,0:T(8,128)} async-done(((f32[1024,256]{1,0:T(8,128)}), f32[128,256]{1,0:T(8,128)}) %reduce-scatter.8.cloned.1.call-update) | async-done | bytes 131088 | tf_op jit(solution)/shard_map/reduce_scatter | solution.py:42
  186.8 1.0 multiply_reduce_fusion
  187.8 1.0 fusion.19
  188.8 0.7 pad_maximum_fusion
  (12 shorter events, 0.2 us)
Async XLA Ops:
  7.2 17.6 %copy-start = (f32[16,128,128]{2,1,0:T(8,128)S(1)}, f32[16,128,128]{2,1,0:T(8,128)}, u32[]{:S(2)}) copy-start(f32[16,128,128]{2,1,0:T(8,128)} %param.11) | copy-start | bytes 3145732
  7.2 10.2 %copy-start.3 = (s32[16]{0:T(128)S(1)}, s32[16]{0:T(128)}, u32[]{:S(2)}) copy-start(s32[16]{0:T(128)} %param.12) | copy-start | bytes 196
  7.2 61.7 %reduce-scatter.4.cloned.1.call-start = ((), (), s32[]{:S(2)}) async-start(), calls=%async_computation.3 | async-start | bytes 1179648 | tf_op jit(solution)/shard_map/reduce_scatter | solution.py:42
  8.9 15.9 %copy-start.2 = (bf16[128,256]{1,0:T(8,128)(2,1)}, bf16[128,256]{1,0:T(8,128)(2,1)S(1)}, u32[]{:S(2)}) copy-start(bf16[128,256]{1,0:T(8,128)(2,1)S(1)} %multiply_convert_fusion.4) | copy-start | bytes 196612
  8.9 5.4 %collective-permute-start = (bf16[128,256]{1,0:T(8,128)(2,1)S(1)}, bf16[128,256]{1,0:T(8,128)(2,1)S(1)}, u32[]{:S(2)}, u32[]{:S(2)}) collective-permute-start(bf16[128,256]{1,0:T(8,128)(2,1)S(1)} %multiply_convert_fusion.4), channel_id=1, source_target_pairs={{0,1},{1,0},{2,3},{3,2},{4,5},{5,4},{6,7},{7,6},{8,9},{9,8},{10,11... | collective-permute-start | bytes 196616 | tf_op jit(solution)/shard_map/ppermute | solution.py:13
  14.3 8.3 %collective-permute-start.1 = (bf16[256,256]{1,0:T(8,128)(2,1)S(1)}, bf16[256,256]{1,0:T(8,128)(2,1)S(1)}, u32[]{:S(2)}, u32[]{:S(2)}) collective-permute-start(bf16[256,256]{1,0:T(8,128)(2,1)S(1)} %maximum_select_fusion.3), channel_id=1, source_target_pairs={{0,2},{1,3},{2,0},{3,1},{4,6},{5,7},{6,4},{7,5},{8,10},{9,11},{10,... | collective-permute-start | bytes 393224 | tf_op jit(solution)/shard_map/ppermute | solution.py:13
  30.2 38.6 %copy-start.1 = (bf16[3,128,256]{2,1,0:T(8,128)(2,1)S(1)}, bf16[3,128,256]{2,1,0:T(8,128)(2,1)}, u32[]{:S(2)}) copy-start(bf16[3,128,256]{2,1,0:T(8,128)(2,1)} %param.13) | copy-start | bytes 589828
  31.6 96.2 %reduce-scatter.6.cloned.1.call-start = ((), (), s32[]{:S(2)}) async-start(), calls=%async_computation.4 | async-start | bytes 1179648 | tf_op jit(solution)/shard_map/reduce_scatter | solution.py:42
  70.9 4.3 %collective-permute-start.2 = (bf16[128,256]{1,0:T(8,128)(2,1)S(1)}, bf16[128,256]{1,0:T(8,128)(2,1)S(1)}, u32[]{:S(2)}, u32[]{:S(2)}) collective-permute-start(bf16[128,256]{1,0:T(8,128)(2,1)S(1)} %multiply_convert_fusion.3), channel_id=1, source_target_pairs={{0,1},{1,0},{2,3},{3,2},{4,5},{5,4},{6,7},{7,6},{8,9},{9,8},{10,11... | collective-permute-start | bytes 196616 | tf_op jit(solution)/shard_map/ppermute | solution.py:13
  75.2 7.5 %collective-permute-start.3 = (bf16[256,256]{1,0:T(8,128)(2,1)S(1)}, bf16[256,256]{1,0:T(8,128)(2,1)S(1)}, u32[]{:S(2)}, u32[]{:S(2)}) collective-permute-start(bf16[256,256]{1,0:T(8,128)(2,1)S(1)} %maximum_select_fusion.4), channel_id=1, source_target_pairs={{0,2},{1,3},{2,0},{3,1},{4,6},{5,7},{6,4},{7,5},{8,10},{9,11},{10,... | collective-permute-start | bytes 393224 | tf_op jit(solution)/shard_map/ppermute | solution.py:13
  91.7 95.0 %reduce-scatter.8.cloned.1.call-start = ((), (), s32[]{:S(2)}) async-start(), calls=%async_computation.5 | async-start | bytes 1179648 | tf_op jit(solution)/shard_map/reduce_scatter | solution.py:42
  129.9 4.3 %collective-permute-start.4 = (bf16[128,256]{1,0:T(8,128)(2,1)S(1)}, bf16[128,256]{1,0:T(8,128)(2,1)S(1)}, u32[]{:S(2)}, u32[]{:S(2)}) collective-permute-start(bf16[128,256]{1,0:T(8,128)(2,1)S(1)} %multiply_convert_fusion.2), channel_id=1, source_target_pairs={{0,1},{1,0},{2,3},{3,2},{4,5},{5,4},{6,7},{7,6},{8,9},{9,8},{10,11... | collective-permute-start | bytes 196616 | tf_op jit(solution)/shard_map/ppermute | solution.py:13
  134.2 7.5 %collective-permute-start.5 = (bf16[256,256]{1,0:T(8,128)(2,1)S(1)}, bf16[256,256]{1,0:T(8,128)(2,1)S(1)}, u32[]{:S(2)}, u32[]{:S(2)}) collective-permute-start(bf16[256,256]{1,0:T(8,128)(2,1)S(1)} %maximum_select_fusion.5), channel_id=1, source_target_pairs={{0,2},{1,3},{2,0},{3,1},{4,6},{5,7},{6,4},{7,5},{8,10},{9,11},{10,... | collective-permute-start | bytes 393224 | tf_op jit(solution)/shard_map/ppermute | solution.py:13
Sparse Core Ops, SparseCore 0:
  31.7 37.1 reduce-scatter.3
  91.9 35.9 reduce-scatter.5
  150.8 35.8 reduce-scatter.7
